TPU v7x, 128 devices: a whole 4x4x4 slice. The times are simulated.
128 devices in a mesh: sa: 4 (over x), sb: 2 (over core), sc: 16 (over z, y).
Axes of the slice: x: 4, y: 4, z: 4, core: 2. Of those that a mesh axis runs over, the one named last changes fastest.
Arguments:
- queries: float32 [65536, 2048], P(('sa', 'sb', 'sc')), may hold values from -6 to 6
- key_rows: float32 [65536, 2048], P(('sa', 'sb', 'sc')), may hold values from -6 to 6
- value_rows: float32 [65536, 2048], P(('sa', 'sb', 'sc')), may hold values from -6 to 6
- out_grad: float32 [65536, 2048], P(('sa', 'sb', 'sc')), may hold values from -6 to 6
- prefix_state: float32 [16, 128, 128], replicated, may hold values from -1536 to 1536
- suffix_state: float32 [16, 128, 128], replicated, may hold values from -1536 to 1536
Outputs:
- query_grad: bfloat16 [65536, 2048], P(('sa', 'sb', 'sc'))
- key_grad: bfloat16 [65536, 2048], P(('sa', 'sb', 'sc'))
- value_grad: bfloat16 [65536, 2048], P(('sa', 'sb', 'sc'))
All inputs are finite; a program needn't handle non-finite values.
Results may differ from a plain program's by a relative error of at most 0.0019.
Values sent between devices are 32-bit elements; how exact they have to be, the bound alone decides.
A program may use at most 576 MiB of HBM per device.

v0:
```python
import math
import jax
import jax.numpy as jnp
from jax import lax
from jax.sharding import PartitionSpec as P


def entering(part, axis, combine, identity):
    place = lax.axis_index(axis)
    gathered = jax.tree.map(lambda a: lax.all_gather(a, axis), part)
    state = jax.tree.map(lambda a, e: jnp.zeros_like(a) + jnp.asarray(e, a.dtype), part, identity)

    def one(hop, state):
        return combine(
            state, jax.tree.map(lambda a: lax.dynamic_index_in_dim(a, hop, 0, False), gathered)
        )

    return lax.fori_loop(0, place, one, state)


def add_states(earlier, later):
    return jax.tree.map(lambda left, right: left + right, earlier, later)


def run_chain(local_terms):
    zero_state = jax.tree.map(jnp.zeros_like, local_terms)
    inner_part = entering(local_terms, "sc", add_states, zero_state)
    group_sum = lax.psum((local_terms[0], local_terms[1]), "sc")
    middle_part = entering(group_sum, "sb", add_states, zero_state)
    block_sum = lax.psum((group_sum[0], group_sum[1]), "sb")
    outer_part = entering(block_sum, "sa", add_states, zero_state)
    return add_states(add_states(outer_part, middle_part), inner_part)


def shards(queries, key_rows, value_rows, out_grad, prefix_state, suffix_state):
    row_count = queries.shape[0]
    head_count = prefix_state.shape[0]
    head_size = prefix_state.shape[1]
    device_count = lax.axis_size("sa") * lax.axis_size("sb") * lax.axis_size("sc")
    factor = 1.0 / math.sqrt(head_size * row_count * device_count)
    highest = lax.Precision.HIGHEST
    shaped = (row_count, head_count, head_size)
    query_t = queries.reshape(shaped)
    key_t = key_rows.reshape(shaped)
    value_t = value_rows.reshape(shaped)
    grad_t = out_grad.reshape(shaped)
    kv_local = jnp.einsum("thd,the->hde", key_t, value_t, precision=highest)
    grad_local = jnp.einsum("the,thd->hed", grad_t, query_t, precision=highest)
    prior_kv, prior_grad = run_chain((kv_local, grad_local))
    total_grad = lax.psum(grad_local, ("sa", "sb", "sc"))
    state_before = prefix_state + prior_kv
    state_after = suffix_state + (total_grad - prior_grad - grad_local)
    lower = (
        lax.broadcasted_iota(jnp.int32, (row_count, row_count), 0)
        >= lax.broadcasted_iota(jnp.int32, (row_count, row_count), 1)
    ).astype(jnp.float32)
    grad_scores = jnp.einsum("the,she->hts", grad_t, value_t, precision=highest) * lower
    attn_scores = jnp.einsum("thd,shd->hts", query_t, key_t, precision=highest) * lower
    query_grad = factor * (
        jnp.einsum("the,hde->thd", grad_t, state_before, precision=highest)
        + jnp.einsum("hts,shd->thd", grad_scores, key_t, precision=highest)
    )
    key_grad = factor * (
        jnp.einsum("she,hed->shd", value_t, state_after, precision=highest)
        + jnp.einsum("hts,thd->shd", grad_scores, query_t, precision=highest)
    )
    value_grad = factor * (
        jnp.einsum("shd,hed->she", key_t, state_after, precision=highest)
        + jnp.einsum("hts,the->she", attn_scores, grad_t, precision=highest)
    )
    flat = (row_count, head_count * head_size)
    return (
        query_grad.astype(jnp.bfloat16).reshape(flat),
        key_grad.astype(jnp.bfloat16).reshape(flat),
        value_grad.astype(jnp.bfloat16).reshape(flat),
    )


def solution(mesh):
    return jax.shard_map(
        shards,
        mesh=mesh,
        in_specs=(
            P(("sa", "sb", "sc"), None),
            P(("sa", "sb", "sc"), None),
            P(("sa", "sb", "sc"), None),
            P(("sa", "sb", "sc"), None),
            P(),
            P(),
        ),
        out_specs=(
            P(("sa", "sb", "sc"), None),
            P(("sa", "sb", "sc"), None),
            P(("sa", "sb", "sc"), None),
        ),
        check_vma=False,
    )
```

profile of v0, /device:TPU:1, one launch (start us, length us, event | category | flops | bytes accessed | tf_op | source)
XLA Modules:
  0.0 613.8 jit_solution(8954921210702635121)
XLA Ops:
  8.0 0.0 all-gather.19.cloned.1.call-start
  8.0 11.2 %fusion.21 = f32[16,128,128]{2,1,0:T(8,128)} fusion(f32[512,2048]{1,0:T(8,128)} %param.14, f32[512,2048]{1,0:T(8,128)} %param.13), kind=kOutput, calls=%fused_computation.27 | convolution fusion | flops 1610612736 | bytes 9437184 | tf_op jit(solution)/shard_map/thd,the->hde/dot_general | solution.py:47
  19.2 0.0 all-gather.19.cloned.1.call-update
  19.2 5.1 copy.46
  24.3 5.7 copy.27
  30.1 9.2 %fusion.16 = f32[16,128,128]{2,1,0:T(8,128)} fusion(f32[512,16,128]{0,2,1:T(8,128)} %copy.27, f32[512,2048]{1,0:T(8,128)} %param.12), kind=kOutput, calls=%fused_computation.22 | convolution fusion | flops 1610612736 | bytes 9437184 | tf_op jit(solution)/shard_map/the,thd->hed/dot_general | solution.py:48
  39.3 94.8 %all-gather.19.cloned.1.call-done = f32[256,128,128]{2,1,0:T(8,128)} async-done(((f32[16,128,128]{2,1,0:T(8,128)}), f32[256,128,128]{2,1,0:T(8,128)}) %all-gather.19.cloned.1.call-update) | async-done | bytes 16777232 | tf_op jit(solution)/shard_map/all_gather | solution.py:10
  134.0 0.0 all-reduce.8.cloned.1.call-start
  134.0 0.7 all-reduce.8.cloned.1.call-update
  134.8 0.0 all-gather.15.cloned.1.call-start
  134.8 93.1 %all-reduce.8.cloned.1.call-done = (f32[16,128,128]{2,1,0:T(8,128)}, f32[16,128,128]{2,1,0:T(8,128)}) async-done(((f32[16,128,128]{2,1,0:T(8,128)}, f32[16,128,128]{2,1,0:T(8,128)}), (f32[16,128,128]{2,1,0:T(8,128)}, f32[16,128,128]{2,1,0:T(8,128)})) %all-reduce.8.cloned.1.call-update) | async-done | bytes 2097168 | tf_op jit(solution)/shard_map/psum | solution.py:28
  227.9 0.0 all-gather.15.cloned.1.call-update
  228.0 0.0 all-gather.17.cloned.1.call-start
  228.0 0.5 all-gather.17.cloned.1.call-update
  228.5 15.4 %all-gather.15.cloned.1.call-done = f32[32,128,128]{2,1,0:T(8,128)} async-done(((f32[16,128,128]{2,1,0:T(8,128)}), f32[32,128,128]{2,1,0:T(8,128)}) %all-gather.15.cloned.1.call-update) | async-done | bytes 2097168 | tf_op jit(solution)/shard_map/all_gather | solution.py:10
  243.9 16.3 %all-gather.17.cloned.1.call-done = f32[32,128,128]{2,1,0:T(8,128)} async-done(((f32[16,128,128]{2,1,0:T(8,128)}), f32[32,128,128]{2,1,0:T(8,128)}) %all-gather.17.cloned.1.call-update) | async-done | bytes 2097168 | tf_op jit(solution)/shard_map/all_gather | solution.py:10
  260.2 0.0 all-reduce.10.cloned.1.call-start
  260.2 0.6 all-reduce.10.cloned.1.call-update
  260.8 0.0 all-gather.21.cloned.1.call-start
  260.8 0.5 all-gather.21.cloned.1.call-update
  261.4 0.0 all-gather.11.cloned.1.call-start
  261.4 30.2 %all-reduce.10.cloned.1.call-done = (f32[1,16,128,128]{3,2,1,0:T(8,128)}, f32[1,16,128,128]{3,2,1,0:T(8,128)}) async-done(((f32[1,16,128,128]{3,2,1,0:T(8,128)}, f32[1,16,128,128]{3,2,1,0:T(8,128)}), (f32[1,16,128,128]{3,2,1,0:T(8,128)}, f32[1,16,128,128]{3,2,1,0:T(8,128)})) %all-reduce.10.cloned.1.call-update) | async-done | bytes 2097168 | tf_op jit(solution)/shard_map/psum | solution.py:30
  291.6 0.0 all-gather.11.cloned.1.call-update
  291.6 0.0 all-gather.13.cloned.1.call-start
  291.6 0.7 all-gather.13.cloned.1.call-update
  292.3 0.0 all-reduce.6.cloned.1.call-start
  292.4 0.5 all-reduce.6.cloned.1.call-update
  292.9 0.1 fusion.55
  293.0 0.0 copy-start.6
  293.1 0.0 copy-start.4
  293.1 0.0 copy-start.5
  293.1 19.5 %fusion.14 = f32[16,512,512]{2,1,0:T(8,128)} fusion(f32[512,2048]{1,0:T(8,128)} %param.12, f32[512,2048]{1,0:T(8,128)} %param.13), kind=kOutput, calls=%fused_computation.20 | convolution fusion | flops 6442450944 | bytes 25165824 | tf_op jit(solution)/shard_map/thd,shd->hts/dot_general | solution.py:58
  312.6 0.0 copy-done.4
  312.6 0.0 copy-done.5
  312.6 14.5 %fusion.11 = f32[16,512,512]{2,1,0:T(8,128)S(1)} fusion(f32[512,2048]{1,0:T(8,128)S(1)} %copy-done.4, f32[512,2048]{1,0:T(8,128)S(1)} %copy-done.5), kind=kOutput, calls=%fused_computation.17 | convolution fusion | flops 6442450944 | bytes 25165824 | tf_op jit(solution)/shard_map/the,she->hts/dot_general | solution.py:57
  327.1 14.5 %fusion.2 = f32[16,512,128]{1,2,0:T(8,128)} fusion(f32[16,512,512]{2,1,0:T(8,128)S(1)} %fusion.11, f32[512,512]{1,0:T(8,128)S(1)} %fusion.55, f32[512,2048]{1,0:T(8,128)} %param.12), kind=kOutput, calls=%fused_computation.8 | convolution fusion | flops 6446645248 | bytes 26214400 | tf_op jit(solution)/shard_map/hts,thd->shd/dot_general | solution.py:65
  341.6 0.0 copy-done.6
  341.6 21.3 %fusion.4 = f32[16,512,128]{1,2,0:T(8,128)} fusion(f32[16,512,512]{2,1,0:T(8,128)S(1)} %fusion.11, f32[512,512]{1,0:T(8,128)S(1)} %fusion.55, f32[512,2048]{1,0:T(8,128)} %param.13), kind=kOutput, calls=%fused_computation.10 | convolution fusion | flops 6446645248 | bytes 26214400 | tf_op jit(solution)/shard_map/hts,shd->thd/dot_general | solution.py:61
  362.9 44.5 %all-gather.21.cloned.1.call-done = f32[256,128,128]{2,1,0:T(8,128)} async-done(((f32[16,128,128]{2,1,0:T(8,128)}), f32[256,128,128]{2,1,0:T(8,128)}) %all-gather.21.cloned.1.call-update) | async-done | bytes 16777232 | tf_op jit(solution)/shard_map/all_gather | solution.py:10
  407.4 0.1 broadcast.6.clone
  407.5 0.1 broadcast.6.clone.1
  407.6 0.0 copy-start.1
  407.6 1.0 copy-done.1
  408.6 0.1 broadcast.6.clone.4
  408.7 0.1 broadcast.6.clone.5
  408.8 2.1 while.37
  408.8 2.1 bitcast_add_fusion.13
  410.9 0.0 copy-start.2
  410.9 45.8 %all-gather.11.cloned.1.call-done = f32[4,16,128,128]{3,2,1,0:T(8,128)} async-done(((f32[1,16,128,128]{3,2,1,0:T(8,128)}), f32[4,16,128,128]{3,2,1,0:T(8,128)}) %all-gather.11.cloned.1.call-update) | async-done | bytes 4194320 | tf_op jit(solution)/shard_map/all_gather | solution.py:10
  456.7 0.0 copy-done.2
  456.7 50.5 %all-gather.13.cloned.1.call-done = f32[4,16,128,128]{3,2,1,0:T(8,128)} async-done(((f32[1,16,128,128]{3,2,1,0:T(8,128)}), f32[4,16,128,128]{3,2,1,0:T(8,128)}) %all-gather.13.cloned.1.call-update) | async-done | bytes 4194320 | tf_op jit(solution)/shard_map/all_gather | solution.py:10
  507.2 0.1 broadcast.6.clone.2
  507.3 1.1 broadcast.6.clone.3
  508.4 44.6 %all-reduce.6.cloned.1.call-done = f32[16,128,128]{2,1,0:T(8,128)} async-done(((f32[16,128,128]{2,1,0:T(8,128)}), f32[16,128,128]{2,1,0:T(8,128)}) %all-reduce.6.cloned.1.call-update) | async-done | bytes 1048592 | tf_op jit(solution)/shard_map/psum | solution.py:50
  552.9 3.5 subtract_add_fusion
  556.4 0.0 copy-start.8
  556.4 1.0 copy-done.8
  557.5 3.8 fusion.23
  561.3 14.6 %fusion.29 = bf16[512,16,128]{0,2,1:T(8,128)(2,1)} fusion(f32[16,128,512]{2,1,0:T(8,128)S(1)} %fusion.23, f32[512,16,128]{0,2,1:T(8,128)S(1)} %copy-done.3, f32[16,512,512]{2,1,0:T(8,128)} %fusion.14, f32[512,512]{1,0:T(8,128)S(1)} %copy-done.7), kind=kOutput, calls=%fused_computation.36 | convolution fusion | flops 6449790976 | bytes 28311552 | tf_op jit(solution)/shard_map/hts,the->she/dot_general | solution.py:69
  575.9 3.9 copy.40
  579.8 9.2 %fusion.31 = bf16[512,16,128]{0,2,1:T(8,128)(2,1)} fusion(f32[16,512,128]{1,2,0:T(8,128)} %fusion.2, f32[16,128,128]{2,1,0:T(8,128)} %copy-done.8, f32[512,2048]{1,0:T(8,128)} %param.14), kind=kOutput, calls=%fused_computation.39 | convolution fusion | flops 1613758464 | bytes 11534336 | tf_op jit(solution)/shard_map/she,hed->shd/dot_general | solution.py:64
  589.0 4.1 copy.39
  593.1 9.2 %fusion.33 = bf16[512,16,128]{0,2,1:T(8,128)(2,1)} fusion(f32[16,512,128]{1,2,0:T(8,128)} %fusion.4, f32[16,128,128]{2,1,0:T(8,128)} %param.16, f32[16,128,128]{2,1,0:T(8,128)S(1)} %get-tuple-element.107, f32[16,128,128]{2,1,0:T(8,128)S(1)} %get-tuple-element.105, f32[16,128,128]{2,1,0:T(8,128)S(1)} %get-tuple-element.106, f32[512,2048]{1,0:T(8,128)} %param.15), kind=kOutput, calls=%fused_computation.42 | convolution fusion | flops 1614544896 | bytes 14680064 | tf_op jit(solution)/shard_map/the,hde->thd/dot_general | solution.py:60
  602.3 3.9 copy.38
  (8 shorter events, 0.0 us)
Async XLA Ops:
  8.0 126.0 %all-gather.19.cloned.1.call-start = ((), (), s32[]{:S(2)}) async-start(), calls=%async_computation.5 | async-start | bytes 17825792 | tf_op jit(solution)/shard_map/all_gather | solution.py:10
  134.0 93.9 %all-reduce.8.cloned.1.call-start = ((), (), s32[]{:S(2)}) async-start(), calls=%async_computation.7 | async-start | bytes 4194304 | tf_op jit(solution)/shard_map/psum | solution.py:28
  134.8 109.2 %all-gather.15.cloned.1.call-start = ((), (), s32[]{:S(2)}) async-start(), calls=%async_computation.3 | async-start | bytes 3145728 | tf_op jit(solution)/shard_map/all_gather | solution.py:10
  228.0 32.2 %all-gather.17.cloned.1.call-start = ((), (), s32[]{:S(2)}) async-start(), calls=%async_computation.4 | async-start | bytes 3145728 | tf_op jit(solution)/shard_map/all_gather | solution.py:10
  260.2 31.4 %all-reduce.10.cloned.1.call-start = ((), (), s32[]{:S(2)}) async-start(), calls=%async_computation.8 | async-start | bytes 4194304 | tf_op jit(solution)/shard_map/psum | solution.py:30
  260.8 146.6 %all-gather.21.cloned.1.call-start = ((), (), s32[]{:S(2)}) async-start(), calls=%async_computation.6 | async-start | bytes 17825792 | tf_op jit(solution)/shard_map/all_gather | solution.py:10
  261.4 195.3 %all-gather.11.cloned.1.call-start = ((), (), s32[]{:S(2)}) async-start(), calls=%async_computation | async-start | bytes 5242880 | tf_op jit(solution)/shard_map/all_gather | solution.py:10
  291.6 215.6 %all-gather.13.cloned.1.call-start = ((), (), s32[]{:S(2)}) async-start(), calls=%async_computation.1 | async-start | bytes 5242880 | tf_op jit(solution)/shard_map/all_gather | solution.py:10
  292.3 260.6 %all-reduce.6.cloned.1.call-start = ((), (), s32[]{:S(2)}) async-start(), calls=%async_computation.2 | async-start | bytes 2097152 | tf_op jit(solution)/shard_map/psum | solution.py:50
  293.0 48.6 %copy-start.6 = (f32[512,512]{1,0:T(8,128)}, f32[512,512]{1,0:T(8,128)S(1)}, u32[]{:S(2)}) copy-start(f32[512,512]{1,0:T(8,128)S(1)} %fusion.55) | copy-start | bytes 3145732
  293.1 19.6 %copy-start.4 = (f32[512,2048]{1,0:T(8,128)S(1)}, f32[512,2048]{1,0:T(8,128)}, u32[]{:S(2)}) copy-start(f32[512,2048]{1,0:T(8,128)} %param.15) | copy-start | bytes 12582916
  293.1 19.6 %copy-start.5 = (f32[512,2048]{1,0:T(8,128)S(1)}, f32[512,2048]{1,0:T(8,128)}, u32[]{:S(2)}) copy-start(f32[512,2048]{1,0:T(8,128)} %param.14) | copy-start | bytes 12582916
  407.6 1.0 copy-start.1
  410.9 45.8 %copy-start.2 = (f32[16,128,128]{2,1,0:T(8,128)}, f32[16,128,128]{2,1,0:T(8,128)S(1)}, u32[]{:S(2)}) copy-start(f32[16,128,128]{2,1,0:T(8,128)S(1)} %get-tuple-element.109) | copy-start | bytes 3145732
  552.9 4.5 copy-start
  556.4 1.0 copy-start.8
  557.5 3.8 copy-start.3
  557.5 3.8 copy-start.7
Sparse Core Ops, SparseCore 0:
  19.4 114.6 all-gather.18
  138.8 89.0 all-reduce.7
  229.7 14.2 all-gather.14
  245.5 14.6 all-gather.16
  263.4 28.1 all-reduce.9
  294.1 113.1 all-gather.20
  409.0 47.6 all-gather.10
  458.3 48.7 all-gather.12
Sparse Core Ops, SparseCore 1:
  298.2 254.7 all-reduce.5
where the time goes:
time: 621 us; the launch traced here: 614 us
  waiting for transfers between devices  439 us (71%)
  matrix products  127 us (20%)
  local copies, waits for them, and re-layouts  26.3 us (4%)
  between operations  16 us (3%)
    all_gather x6, waiting for transfers between devices, entering(): gathered = jax.tree.map(lambda a: lax.all_gather(a, axis), part)  267 us
    psum x1, waiting for transfers between devices, run_chain(): group_sum = lax.psum((local_terms[0], local_terms[1]), 'sc')  93.1 us
    psum x1, waiting for transfers between devices, shards(): total_grad = lax.psum(grad_local, ('sa', 'sb', 'sc'))  44.6 us
    psum x1, waiting for transfers between devices, run_chain(): block_sum = lax.psum((group_sum[0], group_sum[1]), 'sb')  30.2 us
    dot_general x1, matrix products, shards(): jnp.einsum('hts,shd->thd', grad_scores, key_t, precision=highest)  21.3 us
    dot_general x1, matrix products, shards(): jnp.einsum('thd,shd->hts', query_t, key_t, precision=highest) * lower  19.5 us
    unnamed x22, local copies, waits for them, and re-layouts  19 us
    dot_general x1, matrix products, shards(): jnp.einsum('hts,the->she', attn_scores, grad_t, precision=highest)  14.6 us
  transfers between devices with their start and end apart: 9, of which 9 were waited for; matrix products, arithmetic and copies ran while one was open for 15% of the time, Pallas kernels for 0%

commit v1 on v0

--- a/solution.py
+++ b/solution.py
@@ -47,7 +47,7 @@
     kv_local = jnp.einsum("thd,the->hde", key_t, value_t, precision=highest)
     grad_local = jnp.einsum("the,thd->hed", grad_t, query_t, precision=highest)
     prior_kv, prior_grad = run_chain((kv_local, grad_local))
-    total_grad = lax.psum(grad_local, ("sa", "sb", "sc"))
+    total_grad = jnp.sum(lax.all_gather(grad_local, ("sa", "sb", "sc")), axis=0)
     state_before = prefix_state + prior_kv
     state_after = suffix_state + (total_grad - prior_grad - grad_local)
     lower = (

time: 621 us -> 882 us (1.42)
  waiting for transfers between devices: 439 us -> 667 us
  other arithmetic: 5.71 us -> 46.3 us
    all_gather x0 -> x1, waiting for transfers between devices: none -> 274 us  [shards(): total_grad = jnp.sum(lax.all_gather(grad_local, ('sa', 'sb', 'sc')), axis=0)]
    psum x1 -> x0, waiting for transfers between devices: 44.6 us -> none  [shards(): total_grad = lax.psum(grad_local, ('sa', 'sb', 'sc'))]
    reduce_sum x0 -> x1, other arithmetic: none -> 41.5 us  [shards(): total_grad = jnp.sum(lax.all_gather(grad_local, ('sa', 'sb', 'sc')), axis=0)]
    unnamed x22 -> x30, local copies, waits for them, and re-layouts: 19 us -> 16.2 us
  transfers between devices with their start and end apart: 9 -> 9, of which waited for: 9 -> 9; matrix products, arithmetic and copies ran while one was open for 15% -> 12% of each run, Pallas kernels for 0% -> 0%
where the time goes in v1:
time: 882 us; the launch traced here: 875 us
  waiting for transfers between devices  667 us (76%)
  matrix products  124 us (14%)
  other arithmetic  46.3 us (5%)
  local copies, waits for them, and re-layouts  23.5 us (3%)
  between operations  14.3 us (2%)
    all_gather x1, waiting for transfers between devices, shards(): total_grad = jnp.sum(lax.all_gather(grad_local, ('sa', 'sb', 'sc')), axis=0)  274 us
    all_gather x6, waiting for transfers between devices, entering(): gathered = jax.tree.map(lambda a: lax.all_gather(a, axis), part)  266 us
    psum x1, waiting for transfers between devices, run_chain(): group_sum = lax.psum((local_terms[0], local_terms[1]), 'sc')  93.1 us
    reduce_sum x1, other arithmetic, shards(): total_grad = jnp.sum(lax.all_gather(grad_local, ('sa', 'sb', 'sc')), axis=0)  41.5 us
    psum x1, waiting for transfers between devices, run_chain(): block_sum = lax.psum((group_sum[0], group_sum[1]), 'sb')  30.2 us
    dot_general x1, matrix products, shards(): jnp.einsum('hts,shd->thd', grad_scores, key_t, precision=highest)  20.9 us
    dot_general x1, matrix products, shards(): jnp.einsum('thd,shd->hts', query_t, key_t, precision=highest) * lower  19.5 us
  transfers between devices with their start and end apart: 9, of which 9 were waited for; matrix products, arithmetic and copies ran while one was open for 12% of the time, Pallas kernels for 0%

profile of v1, /device:TPU:1, one launch (start us, length us, event | category | flops | bytes accessed | tf_op | source)
XLA Modules:
  0.0 875.2 jit_solution(5194552236594441276)
XLA Ops:
  7.2 0.0 all-gather.21.cloned.1.call-start
  7.2 11.2 %fusion.21 = f32[16,128,128]{2,1,0:T(8,128)} fusion(f32[512,2048]{1,0:T(8,128)} %param.14, f32[512,2048]{1,0:T(8,128)} %param.13), kind=kOutput, calls=%fused_computation.27 | convolution fusion | flops 1610612736 | bytes 9437184 | tf_op jit(solution)/shard_map/thd,the->hde/dot_general | solution.py:47
  18.4 0.0 all-gather.21.cloned.1.call-update
  18.4 5.2 copy.46
  23.6 5.8 copy.27
  29.3 9.2 %fusion.16 = f32[16,128,128]{2,1,0:T(8,128)} fusion(f32[512,16,128]{0,2,1:T(8,128)} %copy.27, f32[512,2048]{1,0:T(8,128)} %param.12), kind=kOutput, calls=%fused_computation.22 | convolution fusion | flops 1610612736 | bytes 9437184 | tf_op jit(solution)/shard_map/the,thd->hed/dot_general | solution.py:48
  38.6 94.6 %all-gather.21.cloned.1.call-done = f32[256,128,128]{2,1,0:T(8,128)} async-done(((f32[16,128,128]{2,1,0:T(8,128)}), f32[256,128,128]{2,1,0:T(8,128)}) %all-gather.21.cloned.1.call-update) | async-done | bytes 16777232 | tf_op jit(solution)/shard_map/all_gather | solution.py:10
  133.2 0.7 all-reduce.5.cloned.1.call-update
  133.9 0.0 all-gather.17.cloned.1.call-start
  134.0 93.1 %all-reduce.5.cloned.1.call-done = (f32[16,128,128]{2,1,0:T(8,128)}, f32[16,128,128]{2,1,0:T(8,128)}) async-done(((f32[16,128,128]{2,1,0:T(8,128)}, f32[16,128,128]{2,1,0:T(8,128)}), (f32[16,128,128]{2,1,0:T(8,128)}, f32[16,128,128]{2,1,0:T(8,128)})) %all-reduce.5.cloned.1.call-update) | async-done | bytes 2097168 | tf_op jit(solution)/shard_map/psum | solution.py:28
  227.1 0.0 all-gather.17.cloned.1.call-update
  227.1 0.0 all-gather.19.cloned.1.call-start
  227.2 0.5 all-gather.19.cloned.1.call-update
  227.7 15.4 %all-gather.17.cloned.1.call-done = f32[32,128,128]{2,1,0:T(8,128)} async-done(((f32[16,128,128]{2,1,0:T(8,128)}), f32[32,128,128]{2,1,0:T(8,128)}) %all-gather.17.cloned.1.call-update) | async-done | bytes 2097168 | tf_op jit(solution)/shard_map/all_gather | solution.py:10
  243.1 16.3 %all-gather.19.cloned.1.call-done = f32[32,128,128]{2,1,0:T(8,128)} async-done(((f32[16,128,128]{2,1,0:T(8,128)}), f32[32,128,128]{2,1,0:T(8,128)}) %all-gather.19.cloned.1.call-update) | async-done | bytes 2097168 | tf_op jit(solution)/shard_map/all_gather | solution.py:10
  259.4 0.0 all-reduce.7.cloned.1.call-start
  259.4 0.6 all-reduce.7.cloned.1.call-update
  259.9 0.0 all-gather.23.cloned.1.call-start
  260.0 0.5 all-gather.23.cloned.1.call-update
  260.5 0.0 all-gather.13.cloned.1.call-start
  260.6 30.2 %all-reduce.7.cloned.1.call-done = (f32[1,16,128,128]{3,2,1,0:T(8,128)}, f32[1,16,128,128]{3,2,1,0:T(8,128)}) async-done(((f32[1,16,128,128]{3,2,1,0:T(8,128)}, f32[1,16,128,128]{3,2,1,0:T(8,128)}), (f32[1,16,128,128]{3,2,1,0:T(8,128)}, f32[1,16,128,128]{3,2,1,0:T(8,128)})) %all-reduce.7.cloned.1.call-update) | async-done | bytes 2097168 | tf_op jit(solution)/shard_map/psum | solution.py:30
  290.7 0.0 all-gather.13.cloned.1.call-update
  290.8 0.0 all-gather.15.cloned.1.call-start
  290.8 0.7 all-gather.15.cloned.1.call-update
  291.5 0.0 all-gather.25.cloned.1.call-start
  291.6 0.7 all-gather.25.cloned.1.call-update
  292.3 0.1 fusion.55
  292.4 0.0 copy-start.9
  292.4 0.0 copy-start.7
  292.4 0.0 copy-start.8
  292.4 19.5 %fusion.14 = f32[16,512,512]{2,1,0:T(8,128)} fusion(f32[512,2048]{1,0:T(8,128)} %param.12, f32[512,2048]{1,0:T(8,128)} %param.13), kind=kOutput, calls=%fused_computation.20 | convolution fusion | flops 6442450944 | bytes 25165824 | tf_op jit(solution)/shard_map/thd,shd->hts/dot_general | solution.py:58
  311.9 0.0 copy-done.7
  311.9 0.0 copy-done.8
  312.0 14.5 %fusion.11 = f32[16,512,512]{2,1,0:T(8,128)S(1)} fusion(f32[512,2048]{1,0:T(8,128)S(1)} %copy-done.7, f32[512,2048]{1,0:T(8,128)S(1)} %copy-done.8), kind=kOutput, calls=%fused_computation.17 | convolution fusion | flops 6442450944 | bytes 25165824 | tf_op jit(solution)/shard_map/the,she->hts/dot_general | solution.py:57
  326.4 20.9 %fusion.4 = f32[16,512,128]{1,2,0:T(8,128)} fusion(f32[16,512,512]{2,1,0:T(8,128)S(1)} %fusion.11, f32[512,512]{1,0:T(8,128)S(1)} %fusion.55, f32[512,2048]{1,0:T(8,128)} %param.13), kind=kOutput, calls=%fused_computation.10 | convolution fusion | flops 6446645248 | bytes 26214400 | tf_op jit(solution)/shard_map/hts,shd->thd/dot_general | solution.py:61
  347.3 14.9 %fusion.2 = f32[16,512,128]{1,2,0:T(8,128)} fusion(f32[16,512,512]{2,1,0:T(8,128)S(1)} %fusion.11, f32[512,512]{1,0:T(8,128)S(1)} %fusion.55, f32[512,2048]{1,0:T(8,128)} %param.12), kind=kOutput, calls=%fused_computation.8 | convolution fusion | flops 6446645248 | bytes 26214400 | tf_op jit(solution)/shard_map/hts,thd->shd/dot_general | solution.py:65
  362.2 43.5 %all-gather.23.cloned.1.call-done = f32[256,128,128]{2,1,0:T(8,128)} async-done(((f32[16,128,128]{2,1,0:T(8,128)}), f32[256,128,128]{2,1,0:T(8,128)}) %all-gather.23.cloned.1.call-update) | async-done | bytes 16777232 | tf_op jit(solution)/shard_map/all_gather | solution.py:10
  405.7 0.1 broadcast.6.clone
  405.8 0.1 broadcast.6.clone.1
  405.9 0.0 copy-start.1
  405.9 1.0 copy-done.1
  406.9 0.1 broadcast.6.clone.4
  407.0 0.1 broadcast.6.clone.5
  407.1 2.1 while.37
  407.1 2.1 bitcast_add_fusion.13
  409.2 46.0 %all-gather.13.cloned.1.call-done = f32[4,16,128,128]{3,2,1,0:T(8,128)} async-done(((f32[1,16,128,128]{3,2,1,0:T(8,128)}), f32[4,16,128,128]{3,2,1,0:T(8,128)}) %all-gather.13.cloned.1.call-update) | async-done | bytes 4194320 | tf_op jit(solution)/shard_map/all_gather | solution.py:10
  455.2 0.0 copy-done.3
  455.2 50.3 %all-gather.15.cloned.1.call-done = f32[4,16,128,128]{3,2,1,0:T(8,128)} async-done(((f32[1,16,128,128]{3,2,1,0:T(8,128)}), f32[4,16,128,128]{3,2,1,0:T(8,128)}) %all-gather.15.cloned.1.call-update) | async-done | bytes 4194320 | tf_op jit(solution)/shard_map/all_gather | solution.py:10
  505.5 0.1 broadcast.6.clone.2
  505.6 1.1 broadcast.6.clone.3
  506.7 9.1 %fusion.33 = bf16[512,16,128]{0,2,1:T(8,128)(2,1)} fusion(f32[16,512,128]{1,2,0:T(8,128)} %fusion.4, f32[16,128,128]{2,1,0:T(8,128)} %param.16, f32[16,128,128]{2,1,0:T(8,128)S(1)} %get-tuple-element.107, f32[16,128,128]{2,1,0:T(8,128)S(1)} %get-tuple-element.105, f32[16,128,128]{2,1,0:T(8,128)S(1)} %get-tuple-element.106, f32[512,2048]{1,0:T(8,128)} %param.15), kind=kOutput, calls=%fused_computation.42 | convolution fusion | flops 1614544896 | bytes 14680064 | tf_op jit(solution)/shard_map/the,hde->thd/dot_general | solution.py:60
  515.8 4.1 copy.38
  519.9 273.6 %all-gather.25.cloned.1.call-done = f32[2048,128,128]{2,1,0:T(8,128)} async-done(((f32[16,128,128]{2,1,0:T(8,128)}), f32[2048,128,128]{2,1,0:T(8,128)}) %all-gather.25.cloned.1.call-update) | async-done | bytes 134217744 | tf_op jit(solution)/shard_map/all_gather | solution.py:50
  793.5 41.5 %reduce_sum.9 = f32[16,128,128]{2,1,0:T(8,128)} reduce(f32[128,16,128,128]{3,2,1,0:T(8,128)} %bitcast.15, f32[]{:T(128)} %constant.45.clone.1), dimensions={0}, to_apply=%region_10.11 | reduce | flops 33292288 | bytes 135266304 | tf_op jit(solution)/shard_map/reduce_sum | solution.py:50
  835.0 2.5 subtract_add_fusion
  837.6 0.0 copy-start.11
  837.6 1.0 copy-done.11
  838.6 0.0 copy-done
  838.6 3.8 fusion.23
  842.4 13.5 %fusion.29 = bf16[512,16,128]{0,2,1:T(8,128)(2,1)S(1)} fusion(f32[16,128,512]{2,1,0:T(8,128)S(1)} %fusion.23, f32[512,16,128]{0,2,1:T(8,128)S(1)} %copy-done.6, f32[16,512,512]{2,1,0:T(8,128)} %fusion.14, f32[512,512]{1,0:T(8,128)S(1)} %copy-done.10), kind=kOutput, calls=%fused_computation.36 | convolution fusion | flops 6449790976 | bytes 28311552 | tf_op jit(solution)/shard_map/hts,the->she/dot_general | solution.py:69
  855.9 0.0 copy-start.12
  855.9 2.6 copy.40
  858.5 7.6 fusion.31
  866.0 2.4 copy.39
  (17 shorter events, 0.0 us)
Async XLA Ops:
  7.2 126.0 %all-gather.21.cloned.1.call-start = ((), (), s32[]{:S(2)}) async-start(), calls=%async_computation.4 | async-start | bytes 17825792 | tf_op jit(solution)/shard_map/all_gather | solution.py:10
  133.2 93.9 %all-reduce.5.cloned.1.call-start = ((), (), s32[]{:S(2)}) async-start(), calls=%async_computation.7 | async-start | bytes 4194304 | tf_op jit(solution)/shard_map/psum | solution.py:28
  133.9 109.2 %all-gather.17.cloned.1.call-start = ((), (), s32[]{:S(2)}) async-start(), calls=%async_computation.2 | async-start | bytes 3145728 | tf_op jit(solution)/shard_map/all_gather | solution.py:10
  227.1 32.2 %all-gather.19.cloned.1.call-start = ((), (), s32[]{:S(2)}) async-start(), calls=%async_computation.3 | async-start | bytes 3145728 | tf_op jit(solution)/shard_map/all_gather | solution.py:10
  259.4 31.4 %all-reduce.7.cloned.1.call-start = ((), (), s32[]{:S(2)}) async-start(), calls=%async_computation.8 | async-start | bytes 4194304 | tf_op jit(solution)/shard_map/psum | solution.py:30
  259.9 145.7 %all-gather.23.cloned.1.call-start = ((), (), s32[]{:S(2)}) async-start(), calls=%async_computation.5 | async-start | bytes 17825792 | tf_op jit(solution)/shard_map/all_gather | solution.py:10
  260.5 194.7 %all-gather.13.cloned.1.call-start = ((), (), s32[]{:S(2)}) async-start(), calls=%async_computation | async-start | bytes 5242880 | tf_op jit(solution)/shard_map/all_gather | solution.py:10
  290.8 214.7 %all-gather.15.cloned.1.call-start = ((), (), s32[]{:S(2)}) async-start(), calls=%async_computation.1 | async-start | bytes 5242880 | tf_op jit(solution)/shard_map/all_gather | solution.py:10
  291.5 502.0 %all-gather.25.cloned.1.call-start = ((), (), s32[]{:S(2)}) async-start(), calls=%async_computation.6 | async-start | bytes 135266304 | tf_op jit(solution)/shard_map/all_gather | solution.py:50
  292.4 54.9 %copy-start.9 = (f32[512,512]{1,0:T(8,128)}, f32[512,512]{1,0:T(8,128)S(1)}, u32[]{:S(2)}) copy-start(f32[512,512]{1,0:T(8,128)S(1)} %fusion.55) | copy-start | bytes 3145732
  292.4 19.6 %copy-start.7 = (f32[512,2048]{1,0:T(8,128)S(1)}, f32[512,2048]{1,0:T(8,128)}, u32[]{:S(2)}) copy-start(f32[512,2048]{1,0:T(8,128)} %param.15) | copy-start | bytes 12582916
  292.4 19.6 %copy-start.8 = (f32[512,2048]{1,0:T(8,128)S(1)}, f32[512,2048]{1,0:T(8,128)}, u32[]{:S(2)}) copy-start(f32[512,2048]{1,0:T(8,128)} %param.14) | copy-start | bytes 12582916
  405.9 1.0 copy-start.1
  409.2 46.0 %copy-start.3 = (f32[16,128,128]{2,1,0:T(8,128)}, f32[16,128,128]{2,1,0:T(8,128)S(1)}, u32[]{:S(2)}) copy-start(f32[16,128,128]{2,1,0:T(8,128)S(1)} %get-tuple-element.109) | copy-start | bytes 3145732
  793.5 41.5 %copy-start.2 = (f32[16,128,128]{2,1,0:T(8,128)S(1)}, f32[16,128,128]{2,1,0:T(8,128)}, u32[]{:S(2)}) copy-start(f32[16,128,128]{2,1,0:T(8,128)} %copy-done.1) | copy-start | bytes 3145732
  793.5 41.5 %copy-start.4 = (f32[16,128,128]{2,1,0:T(8,128)S(1)}, f32[16,128,128]{2,1,0:T(8,128)}, u32[]{:S(2)}) copy-start(f32[16,128,128]{2,1,0:T(8,128)} %copy-done.3) | copy-start | bytes 3145732
  793.5 41.5 %copy-start.5 = (f32[16,128,128]{2,1,0:T(8,128)S(1)}, f32[16,128,128]{2,1,0:T(8,128)}, u32[]{:S(2)}) copy-start(f32[16,128,128]{2,1,0:T(8,128)} %get-tuple-element.108) | copy-start | bytes 3145732
  835.0 3.5 copy-start
  837.6 1.0 copy-start.11
  838.6 3.8 copy-start.6
  838.6 3.8 copy-start.10
  855.9 2.6 copy-start.12
Sparse Core Ops, SparseCore 0:
  18.5 114.6 all-gather.20
  138.0 89.0 all-reduce.4
  228.9 14.2 all-gather.16
  244.7 14.6 all-gather.18
  262.5 28.1 all-reduce.6
  293.3 112.3 all-gather.22
  407.3 47.8 all-gather.12
  456.9 48.5 all-gather.14
  509.2 284.1 all-gather.24
